TPU v7x, 32 devices: a whole 2x2x4 slice. The times are simulated.
32 devices in a mesh: ctx: 4 (over z), node: 4 (over y, core), local: 2 (over x).
Axes of the slice: x: 2, y: 2, z: 4, core: 2. Of those that a mesh axis runs over, the one named last changes fastest.
Arguments:
- tokens: bfloat16 [1024, 3584], P(('node', 'local'), 'ctx'), may hold values from -6 to 6
- expert_ids: int32 [1024, 4], P(('node', 'local')), may hold values from 0 to 7, as said below
- route_scores: float32 [1024, 4], P(('node', 'local')), may hold values from 0.05 to 1
- w_gate: bfloat16 [8, 3584, 2048], P(('node', 'local'), None, 'ctx'), may hold values from -0.09375 to 0.09375
- w_up: bfloat16 [8, 3584, 2048], P(('node', 'local'), None, 'ctx'), may hold values from -0.09375 to 0.09375
- w_down: bfloat16 [8, 2048, 3584], P(('node', 'local'), None, 'ctx'), may hold values from -0.125 to 0.125
- shared_gate: bfloat16 [3584, 2048], P(None, 'ctx'), may hold values from -0.09375 to 0.09375
- shared_up: bfloat16 [3584, 2048], P(None, 'ctx'), may hold values from -0.09375 to 0.09375
- shared_down: bfloat16 [2048, 3584], P(None, 'ctx'), may hold values from -0.125 to 0.125
Outputs:
- mixed: bfloat16 [1024, 3584], P(('node', 'local'), 'ctx')
Inputs may be any that keep to these rules, and one draw needn't show every extreme that they name: `expert_ids`: each row names 4 different experts: two in each of two different node groups, where expert e lies in group e // 2. In each aligned block of 128 rows (the rows of one index of node+local) no group is named by more than 80 rows and no expert more than 80 times; one group, the same in every block, is named by exactly 80 rows in every block, and one of its experts, the same in every block, exactly 80 times.
All inputs are finite; a program needn't handle non-finite values.
Results may differ from a plain program's by a relative error of at most 0.0064.
Values may be sent and summed in bfloat16 or wider, within the bound.
A program may use at most 64 MiB of HBM per device.

v0:
```python
import jax
import jax.numpy as jnp
from jax import lax
from jax.sharding import PartitionSpec as P

route_scale = 2.5


def matmul(left_side, right_side):
    return jnp.dot(left_side, right_side, preferred_element_type=jnp.float32)


def local(
    tokens, expert_ids, route_scores, w_gate, w_up, w_down, shared_gate, shared_up, shared_down
):
    tok_count = tokens.shape[0]
    feat_local = tokens.shape[1]
    top_count = expert_ids.shape[1]
    group_count = lax.axis_size("node")
    member_count = lax.axis_size("local")
    expert_count = group_count * member_count
    group_cap = (10 * tok_count + 4 * group_count - 1) // (4 * group_count)
    capacity = (2 * group_cap + member_count - 1) // member_count
    slot_total = expert_count * capacity
    gate_local = w_gate[0]
    up_local = w_up[0]
    down_local = w_down[0]
    out_width = down_local.shape[1]
    scaled = route_scale * route_scores / jnp.sum(route_scores, axis=1, keepdims=True)
    gate_weights = lax.optimization_barrier(scaled.astype(jnp.bfloat16)).astype(jnp.float32)
    group_range = jnp.arange(group_count, dtype=jnp.int32)
    group_onehot = (expert_ids // member_count)[:, :, None] == group_range[None, None, :]
    flat_ids = expert_ids.reshape(-1)
    pair_count = flat_ids.shape[0]
    onehot = (flat_ids[:, None] == jnp.arange(expert_count, dtype=jnp.int32)[None, :]).astype(
        jnp.int32
    )
    earlier = jnp.cumsum(onehot, axis=0) - onehot
    ranking = jnp.sum(earlier * onehot, axis=1)
    pair_slot = flat_ids * capacity + ranking
    pair_token = jnp.arange(pair_count, dtype=jnp.int32) // top_count
    matches = pair_slot[None, :] == jnp.arange(slot_total, dtype=jnp.int32)[:, None]
    slot_token = jnp.where(
        jnp.any(matches, axis=1),
        jnp.sum(jnp.where(matches, pair_token[None, :], 0), axis=1),
        tok_count,
    )
    padded_tokens = jnp.concatenate([tokens, jnp.zeros((1, feat_local), tokens.dtype)], axis=0)
    send_rows = padded_tokens[slot_token].reshape(group_count, member_count, capacity * feat_local)
    arrived = lax.all_to_all(
        lax.all_to_all(send_rows, "node", split_axis=0, concat_axis=0, tiled=True),
        "local",
        split_axis=1,
        concat_axis=1,
        tiled=True,
    )
    routed_rows = arrived.reshape(slot_total, feat_local)
    stacked = jnp.concatenate([routed_rows, tokens], axis=0)
    segment = lax.all_gather(stacked, "ctx", axis=1, tiled=True)
    routed_part = segment[:slot_total]
    shared_part = segment[slot_total:]
    gate_routed = matmul(routed_part, gate_local)
    up_routed = matmul(routed_part, up_local)
    gate_shared = matmul(shared_part, shared_gate)
    up_shared = matmul(shared_part, shared_up)
    routed_hidden = (jax.nn.silu(gate_routed) * up_routed).astype(jnp.bfloat16)
    shared_hidden = (jax.nn.silu(gate_shared) * up_shared).astype(jnp.bfloat16)
    hidden_stack = jnp.concatenate([routed_hidden, shared_hidden], axis=0)
    segment = lax.all_gather(hidden_stack, "ctx", axis=1, tiled=True)
    routed_out = matmul(segment[:slot_total], down_local)
    shared_out = matmul(segment[slot_total:], shared_down)
    routed_bf = routed_out.astype(jnp.bfloat16)
    sendback = routed_bf.reshape(group_count, member_count, capacity * out_width)
    returned = lax.all_to_all(
        lax.all_to_all(sendback, "node", split_axis=0, concat_axis=0, tiled=True),
        "local",
        split_axis=1,
        concat_axis=1,
        tiled=True,
    )
    returned = returned.reshape(slot_total, out_width)
    pair_out = returned[pair_slot].reshape(tok_count, top_count, out_width).astype(jnp.float32)
    weighted = gate_weights[:, :, None] * pair_out
    group_sum = jnp.einsum(
        "tkg,tkd->tgd", group_onehot.astype(jnp.float32), weighted, precision=lax.Precision.HIGHEST
    )
    rounded = lax.optimization_barrier(group_sum.astype(jnp.bfloat16)).astype(jnp.float32)
    routed_sum = jnp.sum(rounded, axis=1)
    mixed = shared_out + routed_sum
    return mixed.astype(jnp.bfloat16)


def solution(mesh):
    return jax.shard_map(
        local,
        mesh=mesh,
        in_specs=(
            P(("node", "local"), "ctx"),
            P(("node", "local"), None),
            P(("node", "local"), None),
            P(("node", "local"), None, "ctx"),
            P(("node", "local"), None, "ctx"),
            P(("node", "local"), None, "ctx"),
            P(None, "ctx"),
            P(None, "ctx"),
            P(None, "ctx"),
        ),
        out_specs=P(("node", "local"), "ctx"),
        check_vma=False,
    )
```

profile of v0, /device:TPU:0, one launch (start us, length us, event | category | flops | bytes accessed | tf_op | source)
XLA Modules:
  0.0 292.3 jit_solution(5308196414685565889)
XLA Ops:
  7.6 1.1 reduce-window.6
  9.5 1.0 concatenate.9
  10.5 3.1 %gather_fusion = bf16[640,896]{1,0:T(8,128)(2,1)S(1)} fusion(bf16[129,896]{1,0:T(8,128)(2,1)S(1)} %concatenate.9, s32[1024]{0:T(1024)S(1)} %pad_clamp_fusion.1), kind=kCustom, calls=%fused_computation | custom fusion | bytes 2296320 | tf_op jit(solution)/shard_map/gather | solution.py:49
  14.0 19.6 %all_to_all.20 = bf16[4,2,71680]{2,1,0:T(2,128)(2,1)S(1)} all-to-all(bf16[4,2,71680]{2,1,0:T(2,128)(2,1)S(1)} %reshape.111), channel_id=1, replica_groups=mesh['ctx'=4,'node'=4,'local'=2] {'node'}, dimensions={0} | all-to-all | bytes 2293760 | tf_op jit(solution)/shard_map/all_to_all | solution.py:51
  34.1 17.1 %all_to_all.21 = bf16[4,2,71680]{2,0,1:T(4,128)(2,1)S(1)} all-to-all(bf16[4,2,71680]{2,0,1:T(4,128)(2,1)S(1)} %copy.45), channel_id=1, replica_groups=mesh['ctx'=4,'node'=4,'local'=2] {'local'}, dimensions={1} | all-to-all | bytes 2293760 | tf_op jit(solution)/shard_map/all_to_all | solution.py:50
  51.3 1.2 copy.46
  52.4 0.8 reshape.112
  53.3 1.2 pad_maximum_fusion
  54.6 102.0 %all-gather.3.cloned.1.call-done = bf16[768,3584]{1,0:T(8,128)(2,1)} async-done(((bf16[768,896]{1,0:T(8,128)(2,1)}), bf16[768,3584]{1,0:T(8,128)(2,1)}) %all-gather.3.cloned.1.call-update) | async-done | bytes 5505040 | tf_op jit(solution)/shard_map/all_gather | solution.py:59
  156.6 6.1 %fusion.2 = f32[640,512]{1,0:T(8,128)S(1)} fusion(bf16[768,3584]{1,0:T(8,128)(2,1)} %all-gather.3.cloned.1.call-done, bf16[1,3584,512]{2,1,0:T(8,128)(2,1)} %param.12), kind=kOutput, calls=%fused_computation.4 | convolution fusion | flops 2348810240 | bytes 9568256 | tf_op jit(solution)/shard_map/dot_general | solution.py:10
  163.3 1.4 copy-done.6
  164.7 2.6 fusion.24
  168.0 0.9 pad_maximum_fusion.1
  169.0 61.9 %all-gather.5.cloned.1.call-done = bf16[768,2048]{1,0:T(8,128)(2,1)} async-done(((bf16[768,512]{1,0:T(8,128)(2,1)}), bf16[768,2048]{1,0:T(8,128)(2,1)}) %all-gather.5.cloned.1.call-update) | async-done | bytes 3145744 | tf_op jit(solution)/shard_map/all_gather | solution.py:69
  230.9 5.7 %fusion.11 = bf16[640,896]{1,0:T(8,128)(2,1)S(1)} fusion(bf16[1,2048,896]{2,1,0:T(8,128)(2,1)} %param.14, bf16[768,2048]{1,0:T(8,128)(2,1)} %all-gather.5.cloned.1.call-done), kind=kOutput, calls=%fused_computation.14 | convolution fusion | flops 2349383680 | bytes 7438336 | tf_op jit(solution)/shard_map/dot_general | solution.py:10
  237.0 18.0 %all_to_all.22 = bf16[4,2,71680]{2,1,0:T(2,128)(2,1)S(1)} all-to-all(bf16[4,2,71680]{2,1,0:T(2,128)(2,1)S(1)} %reshape.113), channel_id=1, replica_groups=mesh['ctx'=4,'node'=4,'local'=2] {'node'}, dimensions={0} | all-to-all | bytes 2293760 | tf_op jit(solution)/shard_map/all_to_all | solution.py:75
  255.0 1.6 copy.49
  256.6 3.8 %all-to-all-start.3 = ((bf16[4,2,71680]{2,0,1:T(4,128)(2,1)}), bf16[4,2,71680]{2,0,1:T(4,128)(2,1)S(1)}, u32[]{:S(2)}, u32[]{:S(2)}) async-start(bf16[4,2,71680]{2,0,1:T(4,128)(2,1)} %copy.49), calls=%async_computation.3 | async-start | bytes 2293760 | tf_op jit(solution)/shard_map/all_to_all | solution.py:74
  260.9 13.9 %all-to-all-done.3 = bf16[4,2,71680]{2,0,1:T(4,128)(2,1)S(1)} async-done(((bf16[4,2,71680]{2,0,1:T(4,128)(2,1)}), bf16[4,2,71680]{2,0,1:T(4,128)(2,1)S(1)}, u32[]{:S(2)}, u32[]{:S(2)}) %all-to-all-start.3) | async-done | bytes 1146912 | tf_op jit(solution)/shard_map/all_to_all | solution.py:74
  274.9 1.2 copy.50
  276.9 2.1 gather_fusion.1
  279.4 2.3 fusion.16
  281.7 1.3 convert_reduce_fusion
  283.0 2.5 fusion.30
  (49 shorter events, 6.3 us)
Async XLA Ops:
  6.5 150.0 %all-gather.3.cloned.1.call-start = ((), (), s32[]{:S(2)}) async-start(), calls=%async_computation.4 | async-start | bytes 6881280 | tf_op jit(solution)/shard_map/all_gather | solution.py:59
  51.3 2.0 copy-start.2
  54.5 176.4 %all-gather.5.cloned.1.call-start = ((), (), s32[]{:S(2)}) async-start(), calls=%async_computation.5 | async-start | bytes 3932160 | tf_op jit(solution)/shard_map/all_gather | solution.py:69
  156.6 6.1 %copy-start = (bf16[3584,512]{1,0:T(8,128)(2,1)S(1)}, bf16[3584,512]{1,0:T(8,128)(2,1)}, u32[]{:S(2)}) copy-start(bf16[3584,512]{1,0:T(8,128)(2,1)} %param.15) | copy-start | bytes 11010052
  156.6 6.1 %copy-start.3 = (bf16[768,3584]{1,0:T(8,128)(2,1)S(1)}, bf16[768,3584]{1,0:T(8,128)(2,1)}, u32[]{:S(2)}) copy-start(bf16[768,3584]{1,0:T(8,128)(2,1)} %all-gather.3.cloned.1.call-done) | copy-start | bytes 16515076
  162.7 2.0 copy-start.6
  164.7 2.7 copy-start.7
  255.0 5.4 %copy-start.4 = (s32[128,4]{0,1:T(4,128)S(1)}, s32[128,4]{0,1:T(4,128)}, u32[]{:S(2)}) copy-start(s32[128,4]{0,1:T(4,128)} %param.10) | copy-start | bytes 6148
  255.0 5.7 %copy-start.5 = (f32[128,4]{0,1:T(4,128)S(1)}, f32[128,4]{0,1:T(4,128)}, u32[]{:S(2)}) copy-start(f32[128,4]{0,1:T(4,128)} %param.11) | copy-start | bytes 6148
  256.6 18.3 %all-to-all-start.3 = ((bf16[4,2,71680]{2,0,1:T(4,128)(2,1)}), bf16[4,2,71680]{2,0,1:T(4,128)(2,1)S(1)}, u32[]{:S(2)}, u32[]{:S(2)}) async-start(bf16[4,2,71680]{2,0,1:T(4,128)(2,1)} %copy.49), calls=%async_computation.3 | async-start | bytes 2293760 | tf_op jit(solution)/shard_map/all_to_all | solution.py:74
  279.4 3.6 %copy-start.1 = (bf16[2048,896]{1,0:T(8,128)(2,1)S(1)}, bf16[2048,896]{1,0:T(8,128)(2,1)}, u32[]{:S(2)}) copy-start(bf16[2048,896]{1,0:T(8,128)(2,1)} %param.17) | copy-start | bytes 11010052
Sparse Core Ops, SparseCore 0:
  54.6 101.8 all-gather.2
  169.1 61.7 all-gather.4
where the time goes:
time: 293 us; the launch traced here: 292 us
  waiting for transfers between devices  178 us (61%)
  blocking collectives  54.7 us (19%)
  matrix products  20.5 us (7%)
  local copies, waits for them, and re-layouts  16.5 us (6%)
  between operations  13.7 us (5%)
  other arithmetic  5.24 us (2%)
  starting transfers between devices  3.82 us (1%)
    all_gather x1, waiting for transfers between devices, local(): segment = lax.all_gather(stacked, 'ctx', axis=1, tiled=True)  102 us
    all_gather x1, waiting for transfers between devices, local(): segment = lax.all_gather(hidden_stack, 'ctx', axis=1, tiled=True)  61.9 us
    all_to_all x1, blocking collectives, local(): lax.all_to_all(send_rows, 'node', split_axis=0, concat_axis=0, tiled=True)  19.6 us
    dot_general x6, matrix products, matmul(): return jnp.dot(left_side, right_side, preferred_element_type=jnp.float32)  18.2 us
    all_to_all x1, blocking collectives, local(): lax.all_to_all(sendback, 'node', split_axis=0, concat_axis=0, tiled=True)  18 us
    all_to_all x1, blocking collectives, local(): lax.all_to_all(lax.all_to_all(send_rows, 'node', split_axis=0, concat_axi...  17.1 us
    all_to_all x1, waiting for transfers between devices, local(): lax.all_to_all(lax.all_to_all(sendback, 'node', split_axis=0, concat_axis...  13.9 us
  transfers between devices with their start and end apart: 3, of which 3 were waited for; matrix products, arithmetic and copies ran while one was open for 0% of the time, Pallas kernels for 0%

commit v1 on v0

--- a/solution.py
+++ b/solution.py
@@ -1,9 +1,18 @@
+import functools
 import jax
 import jax.numpy as jnp
 from jax import lax
 from jax.sharding import PartitionSpec as P
 
 route_scale = 2.5
+
+
+def slabs_touch(m, across, dim_no):
+    mixed_arr = lax.all_gather(m, across)
+    return jnp.concatenate(mixed_arr, dim_no)
+
+
+work_threads = functools.partial(slabs_touch, across="ctx", dim_no=1)
 
 
 def matmul(left_side, right_side):
@@ -66,7 +75,7 @@
     routed_hidden = (jax.nn.silu(gate_routed) * up_routed).astype(jnp.bfloat16)
     shared_hidden = (jax.nn.silu(gate_shared) * up_shared).astype(jnp.bfloat16)
     hidden_stack = jnp.concatenate([routed_hidden, shared_hidden], axis=0)
-    segment = lax.all_gather(hidden_stack, "ctx", axis=1, tiled=True)
+    segment = work_threads(hidden_stack)
     routed_out = matmul(segment[:slot_total], down_local)
     shared_out = matmul(segment[slot_total:], shared_down)
     routed_bf = routed_out.astype(jnp.bfloat16)

time: 293 us -> 302 us (1.031)
  local copies, waits for them, and re-layouts: 16.5 us -> 27.1 us
    all_gather x0 -> x1, local copies, waits for them, and re-layouts: none -> 3.18 us  [slabs_touch(): mixed_arr = lax.all_gather(m, across)]
    reshape x1, local copies, waits for them, and re-layouts: 0.36 us -> 3.52 us  [local(): routed_bf.reshape(group_count, member_count, capacity * out_width)]
where the time goes in v1:
time: 302 us; the launch traced here: 301 us
  waiting for transfers between devices  177 us (59%)
  blocking collectives  55.7 us (18%)
  local copies, waits for them, and re-layouts  27.1 us (9%)
  matrix products  17.7 us (6%)
  between operations  13.7 us (5%)
  other arithmetic  5.24 us (2%)
  starting transfers between devices  4.67 us (2%)
    all_gather x1, waiting for transfers between devices, local(): segment = lax.all_gather(stacked, 'ctx', axis=1, tiled=True)  102 us
    all_gather x1, waiting for transfers between devices, slabs_touch(): mixed_arr = lax.all_gather(m, across)  61.9 us
    all_to_all x1, blocking collectives, local(): lax.all_to_all(send_rows, 'node', split_axis=0, concat_axis=0, tiled=True)  19.6 us
    all_to_all x1, blocking collectives, local(): lax.all_to_all(sendback, 'node', split_axis=0, concat_axis=0, tiled=True)  19 us
    all_to_all x1, blocking collectives, local(): lax.all_to_all(lax.all_to_all(send_rows, 'node', split_axis=0, concat_axi...  17.1 us
    dot_general x6, matrix products, matmul(): return jnp.dot(left_side, right_side, preferred_element_type=jnp.float32)  15.4 us
    all_to_all x1, waiting for transfers between devices, local(): lax.all_to_all(lax.all_to_all(sendback, 'node', split_axis=0, concat_axis...  13.2 us
  transfers between devices with their start and end apart: 3, of which 3 were waited for; matrix products, arithmetic and copies ran while one was open for 0% of the time, Pallas kernels for 0%

profile of v1, /device:TPU:0, one launch (start us, length us, event | category | flops | bytes accessed | tf_op | source)
XLA Modules:
  0.0 301.1 jit_solution(10338365601813335526)
XLA Ops:
  7.6 1.1 reduce-window.6
  10.5 3.1 %gather_fusion = bf16[640,896]{1,0:T(8,128)(2,1)S(1)} fusion(bf16[129,896]{1,0:T(8,128)(2,1)S(1)} %concatenate.9, s32[1024]{0:T(1024)S(1)} %pad_clamp_fusion.1), kind=kCustom, calls=%fused_computation | custom fusion | bytes 2296320 | tf_op jit(solution)/shard_map/gather | solution.py:58
  14.0 19.6 %all_to_all.20 = bf16[4,2,71680]{2,1,0:T(2,128)(2,1)S(1)} all-to-all(bf16[4,2,71680]{2,1,0:T(2,128)(2,1)S(1)} %reshape.117), channel_id=1, replica_groups=mesh['ctx'=4,'node'=4,'local'=2] {'node'}, dimensions={0} | all-to-all | bytes 2293760 | tf_op jit(solution)/shard_map/all_to_all | solution.py:60
  34.1 17.1 %all_to_all.21 = bf16[4,2,71680]{2,0,1:T(4,128)(2,1)S(1)} all-to-all(bf16[4,2,71680]{2,0,1:T(4,128)(2,1)S(1)} %copy.49), channel_id=1, replica_groups=mesh['ctx'=4,'node'=4,'local'=2] {'local'}, dimensions={1} | all-to-all | bytes 2293760 | tf_op jit(solution)/shard_map/all_to_all | solution.py:59
  51.3 1.2 copy.50
  53.3 1.2 pad_maximum_fusion
  54.6 102.0 %all-gather.4.cloned.1.call-done = bf16[768,3584]{1,0:T(8,128)(2,1)} async-done(((bf16[768,896]{1,0:T(8,128)(2,1)}), bf16[768,3584]{1,0:T(8,128)(2,1)}) %all-gather.4.cloned.1.call-update) | async-done | bytes 5505040 | tf_op jit(solution)/shard_map/all_gather | solution.py:68
  156.6 6.1 %fusion.2 = f32[640,512]{1,0:T(8,128)S(1)} fusion(bf16[768,3584]{1,0:T(8,128)(2,1)} %all-gather.4.cloned.1.call-done, bf16[1,3584,512]{2,1,0:T(8,128)(2,1)} %param.12), kind=kOutput, calls=%fused_computation.4 | convolution fusion | flops 2348810240 | bytes 9568256 | tf_op jit(solution)/shard_map/dot_general | solution.py:19
  163.3 1.4 copy-done.7
  164.7 2.6 fusion.21
  169.0 61.9 %all-gather.6.cloned.1.call-done = bf16[3072,512]{1,0:T(8,128)(2,1)} async-done(((bf16[768,512]{1,0:T(8,128)(2,1)}), bf16[3072,512]{1,0:T(8,128)(2,1)}) %all-gather.6.cloned.1.call-update) | async-done | bytes 3145744 | tf_op jit(solution)/shard_map/all_gather | solution.py:11
  230.9 3.2 %copy.51 = bf16[4,768,512]{1,2,0:T(8,128)(2,1)S(1)} copy(bf16[4,768,512]{2,1,0:T(8,128)(2,1)} %bitcast.36) | data formatting | bytes 6291456 | tf_op jit(solution)/shard_map/all_gather | solution.py:11
  234.3 1.8 copy-done.9
  236.1 4.0 %fusion.10 = bf16[640,896]{1,0:T(8,128)(2,1)} fusion(bf16[640,2048]{0,1:T(8,128)(2,1)S(1)} %bitcast.37, bf16[1,2048,896]{2,1,0:T(8,128)(2,1)S(1)} %copy-done.9), kind=kOutput, calls=%fused_computation.13 | convolution fusion | flops 2349383680 | bytes 7438336 | tf_op jit(solution)/shard_map/dot_general | solution.py:19
  240.1 3.5 %reshape.120 = bf16[4,2,71680]{2,1,0:T(2,128)(2,1)} reshape(bf16[640,896]{1,0:T(8,128)(2,1)} %fusion.10) | data formatting | bytes 2293760 | tf_op jit(solution)/shard_map/reshape | solution.py:82
  243.6 19.0 %all_to_all.22 = bf16[4,2,71680]{2,1,0:T(2,128)(2,1)S(1)} all-to-all(bf16[4,2,71680]{2,1,0:T(2,128)(2,1)} %reshape.120), channel_id=1, replica_groups=mesh['ctx'=4,'node'=4,'local'=2] {'node'}, dimensions={0} | all-to-all | bytes 2293760 | tf_op jit(solution)/shard_map/all_to_all | solution.py:84
  262.6 1.6 copy.54
  264.2 4.6 %all-to-all-start.3 = ((bf16[4,2,71680]{2,0,1:T(4,128)(2,1)}), bf16[4,2,71680]{2,0,1:T(4,128)(2,1)}, u32[]{:S(2)}, u32[]{:S(2)}) async-start(bf16[4,2,71680]{2,0,1:T(4,128)(2,1)} %copy.54), calls=%async_computation.3 | async-start | bytes 2293760 | tf_op jit(solution)/shard_map/all_to_all | solution.py:83
  270.3 13.2 %all-to-all-done.3 = bf16[4,2,71680]{2,0,1:T(4,128)(2,1)} async-done(((bf16[4,2,71680]{2,0,1:T(4,128)(2,1)}), bf16[4,2,71680]{2,0,1:T(4,128)(2,1)}, u32[]{:S(2)}, u32[]{:S(2)}) %all-to-all-start.3) | async-done | bytes 1146912 | tf_op jit(solution)/shard_map/all_to_all | solution.py:83
  283.4 2.4 copy.55
  286.7 2.1 gather_fusion.1
  289.2 2.3 fusion.13
  291.6 1.3 convert_reduce_fusion
  292.9 1.4 fusion.27
  (56 shorter events, 9.7 us)
Async XLA Ops:
  6.5 150.0 %all-gather.4.cloned.1.call-start = ((), (), s32[]{:S(2)}) async-start(), calls=%async_computation.4 | async-start | bytes 6881280 | tf_op jit(solution)/shard_map/all_gather | solution.py:68
  51.3 2.0 copy-start.3
  54.5 176.4 %all-gather.6.cloned.1.call-start = ((), (), s32[]{:S(2)}) async-start(), calls=%async_computation.5 | async-start | bytes 3932160 | tf_op jit(solution)/shard_map/all_gather | solution.py:11
  156.6 6.1 %copy-start = (bf16[3584,512]{1,0:T(8,128)(2,1)S(1)}, bf16[3584,512]{1,0:T(8,128)(2,1)}, u32[]{:S(2)}) copy-start(bf16[3584,512]{1,0:T(8,128)(2,1)} %param.15) | copy-start | bytes 11010052
  156.6 6.1 %copy-start.4 = (bf16[768,3584]{1,0:T(8,128)(2,1)S(1)}, bf16[768,3584]{1,0:T(8,128)(2,1)}, u32[]{:S(2)}) copy-start(bf16[768,3584]{1,0:T(8,128)(2,1)} %all-gather.4.cloned.1.call-done) | copy-start | bytes 16515076
  162.7 2.0 copy-start.7
  164.7 2.7 copy-start.8
  234.1 2.0 copy-start.9
  262.6 6.3 %copy-start.5 = (s32[128,4]{0,1:T(4,128)S(1)}, s32[128,4]{0,1:T(4,128)}, u32[]{:S(2)}) copy-start(s32[128,4]{0,1:T(4,128)} %param.10) | copy-start | bytes 6148
  262.6 6.6 %copy-start.6 = (f32[128,4]{0,1:T(4,128)S(1)}, f32[128,4]{0,1:T(4,128)}, u32[]{:S(2)}) copy-start(f32[128,4]{0,1:T(4,128)} %param.11) | copy-start | bytes 6148
  264.2 19.2 %all-to-all-start.3 = ((bf16[4,2,71680]{2,0,1:T(4,128)(2,1)}), bf16[4,2,71680]{2,0,1:T(4,128)(2,1)}, u32[]{:S(2)}, u32[]{:S(2)}) async-start(bf16[4,2,71680]{2,0,1:T(4,128)(2,1)} %copy.54), calls=%async_computation.3 | async-start | bytes 2293760 | tf_op jit(solution)/shard_map/all_to_all | solution.py:83
  289.2 3.6 %copy-start.1 = (bf16[2048,896]{1,0:T(8,128)(2,1)S(1)}, bf16[2048,896]{1,0:T(8,128)(2,1)}, u32[]{:S(2)}) copy-start(bf16[2048,896]{1,0:T(8,128)(2,1)} %param.17) | copy-start | bytes 11010052
  289.2 3.6 %copy-start.2 = (bf16[128,4,512]{0,2,1:T(8,128)(2,1)S(1)}, bf16[128,4,512]{0,2,1:T(8,128)(2,1)}, u32[]{:S(2)}) copy-start(bf16[128,4,512]{0,2,1:T(8,128)(2,1)} %slice.39) | copy-start | bytes 1572868
Sparse Core Ops, SparseCore 0:
  54.6 101.8 all-gather.3
  169.1 61.7 all-gather.5
